TPU v7x, 128 devices: a whole 4x4x4 slice. The times are simulated.
128 devices in a mesh: chan: 4 (over y), space: 32 (over x, z, core).
Axes of the slice: x: 4, y: 4, z: 4, core: 2. Of those that a mesh axis runs over, the one named last changes fastest.
Arguments:
- features: bfloat16 [16384, 512], P('space', 'chan'), may hold values from -6 to 6
- positions: float32 [3, 16384], replicated, may hold values from 0 to 8
- pair_first: int32 [512], P('space'), may hold values from 0 to 127, as said below
- pair_second: int32 [512], P('space'), may hold values from 0 to 127, as said below
- pair_counts: int32 [32], P('space'), may hold values from 1 to 16, 384 in all
- wave_index: int32 [3, 1024], replicated, may hold values from -6 to 6, as said below
- radial_weight: bfloat16 [32, 512], P(None, 'chan'), may hold values from -1 to 1
- smearing: float32 [512], P('chan'), may hold values from 0.1 to 0.6
- mix_weight: bfloat16 [512, 512], P(None, 'chan'), may hold values from -0.25 to 0.25
Outputs:
- updated: bfloat16 [16384, 512], P('space', 'chan')
Inputs may be any that keep to these rules, and one draw needn't show every extreme that they name: `pair_first`: slot t belongs to spatial device t // 16; its first block lies on that device, which holds blocks d * 4 onward. `pair_second`: the second blocks of the 16 slots of one spatial device lie on 16 distinct spatial devices. Device d lists its first pair_counts[d] slots; the others are unused. `wave_index`: no wavevector index is the zero vector.
All inputs are finite; a program needn't handle non-finite values.
Results may differ from a plain program's by a relative error of at most 0.0064.
Values may be sent and summed in bfloat16 or wider, within the bound.
A program may use at most 64 MiB of HBM per device.

v0:
```python
import functools
import math

import jax
import jax.numpy as jnp
from jax import lax
from jax.experimental import pallas as pl
from jax.experimental.pallas import tpu as pltpu
from jax.sharding import PartitionSpec as P

BLOCK = 128
NX, NZ, NCORE, NCHAN = 4, 4, 2, 4
NSPACE = NX * NZ * NCORE
ROWS = 512
CH = 128
KV = 1024
NB = 32
MESH = pl.DeviceIdType.MESH
VM = pl.BlockSpec(memory_space=pltpu.VMEM)
SM = pl.BlockSpec(memory_space=pltpu.SMEM)

REACH = 4.0 * math.sqrt(3.0)
STEP = REACH / (NB - 1)
SPREAD = 1.5 * STEP
SCALE = math.sqrt(math.log2(math.e)) / SPREAD
DELTA = STEP * SCALE
GROUP = 8
PER = ROWS // BLOCK

SIN_C = (3.14159264, -5.167710084, 2.550077523, -0.5982912856, 0.0776576603)
COS_C = (0.9999999532, -4.934792831, 4.058411353, -1.331876568, 0.2196896111)


def horner(v, coeffs):
    out = coeffs[-1] * v + coeffs[-2]
    for c in coeffs[-3::-1]:
        out = out * v + c
    return out


def cos_sin_turns(t):
    u = t - jnp.floor(t + 0.5)
    v = u * u
    s = u * horner(v, SIN_C)
    c = horner(v, COS_C)
    s2 = s + s
    return (1.0 - s2 * s).astype(jnp.bfloat16), (s2 * c).astype(jnp.bfloat16)


def remote(src, dst, send, recv, space):
    return pltpu.make_async_remote_copy(
        src_ref=src, dst_ref=dst, send_sem=send, recv_sem=recv,
        device_id={"space": space}, device_id_type=MESH,
    )


def place(x, z, core):
    return (lax.rem(x + 2 * NX, NX) * NZ + lax.rem(z + 2 * NZ, NZ)) * NCORE + core


HALF = ROWS // 2
QUART = ROWS // 4
FULL, LO, HI = (0, HALF), (0, QUART), (QUART, QUART)
EVENTS = (
    (0, 0, FULL, 1, 0), (0, 0, FULL, -1, 0), (0, 0, FULL, 0, 1), (0, 0, FULL, 0, -1),
    (-1, 0, LO, 1, 0), (-1, 0, FULL, 0, 1), (-1, 0, FULL, 0, -1),
    (1, 0, HI, -1, 0), (1, 0, FULL, 0, 1), (1, 0, FULL, 0, -1),
    (-2, 0, LO, 0, 1), (-2, 0, LO, 0, -1), (2, 0, HI, 0, 1), (2, 0, HI, 0, -1),
    (0, -1, LO, 0, 1), (0, 1, HI, 0, -1),
    (-1, -1, LO, 0, 1), (-1, 1, HI, 0, -1), (1, -1, LO, 0, 1), (1, 1, HI, 0, -1),
    (-2, -1, LO, 0, 1), (2, 1, HI, 0, -1),
)
NEV = len(EVENTS)


def expansion(d):
    out = [None] * NB
    half = GROUP // 2
    for c in range(half, NB, GROUP):
        a, b = d - c * DELTA, c * DELTA - d
        mid = jnp.exp2(a * b)
        up, down = jnp.exp2(a * (2.0 * DELTA)), jnp.exp2(b * (2.0 * DELTA))
        out[c] = mid
        e = mid
        for j in range(1, GROUP - half):
            e = e * up
            out[c + j] = e
        e = mid
        for j in range(1, half + 1):
            e = e * down
            out[c - j] = e
    return [e.astype(jnp.bfloat16) for e in out]


def kernel(feat, first, second, count, first_v, second_v, count_v, pos, wave, weight, smear, mix, out,
           g, codes, codes_in, code_s, fg, cs, acc, posb, posq, wt, wb, s_acc, m,
           gs, gr, ks, kr, ps, pr, fs, fr, ms, mr, ls):
    me = lax.axis_index("space")
    yme = lax.axis_index("chan")
    core = lax.rem(me, NCORE)
    chip = me // NCORE
    x, z = chip // NZ, lax.rem(chip, NZ)
    partner = chip * NCORE + (1 - core)
    yup, ydown = lax.rem(yme + 1, NCHAN), lax.rem(yme + NCHAN - 1, NCHAN)
    yacross = lax.rem(yme + 2, NCHAN)

    barrier = pltpu.get_barrier_semaphore()

    @pl.loop(1, NSPACE)
    def _(i):
        pl.semaphore_signal(barrier, inc=1, device_id={"space": lax.rem(me + i, NSPACE)},
                            device_id_type=MESH)
    for peer in (yup, ydown):
        pl.semaphore_signal(barrier, inc=1, device_id={"chan": peer}, device_id_type=MESH)

    own = pltpu.make_async_copy(feat, g.at[pl.ds(me * PER, PER)], ls.at[0])
    own.start()

    sec = second_v[...]
    sec_dev = sec // PER
    code = (sec - sec_dev * PER) * BLOCK + first_v[...] + 1
    slot = lax.broadcasted_iota(jnp.int32, (NSPACE, 16), 1)
    dev = lax.broadcasted_iota(jnp.int32, (NSPACE, 16), 0)
    match = (slot < count_v[...]) & (sec_dev == dev)
    picked = jnp.sum(jnp.where(match, code, 0), axis=1, keepdims=True)
    codes[...] = jnp.broadcast_to(picked, (NSPACE, BLOCK))[:, None, :]

    for k in range(NB):
        j = k % GROUP - GROUP // 2
        row = weight[k:k + 1, :].astype(jnp.float32) * (2.0 ** (-j * j * DELTA * DELTA))
        wb[k] = jnp.broadcast_to(row, (16, CH)).astype(jnp.bfloat16)

    pl.semaphore_wait(barrier, NSPACE - 1 + 2)

    def ev(flow, i):
        da, db, (r0, n), sa, sb = EVENTS[i]
        if flow == 0:
            origin, to = place(x + da, z + db, core), place(x + sa, z + sb, core)
        else:
            origin, to = place(x + db, z + da, core), place(x + sb, z + sa, core)
        first_row = (flow * HALF + r0) // BLOCK
        blocks = g.at[pl.ds(origin * PER + first_row, n // BLOCK)]
        src = feat.at[pl.ds(first_row, n // BLOCK)] if da == 0 and db == 0 else blocks
        return remote(src, blocks, gs.at[flow, i], gr.at[flow, i], to)

    def code_copy(i):
        to = lax.rem(me + i, NSPACE)
        return remote(codes.at[to], codes_in.at[me], ks.at[i], kr.at[i], to)

    def to_partner(c):
        blocks = g.at[pl.ds((c * NCORE + core) * PER, PER)]
        return remote(blocks, blocks, ps.at[c], pr.at[c], partner)

    def start(*events):
        for i in events:
            for flow in (0, 1):
                ev(flow, i).start()

    def arrived(*events):
        for i in events:
            for flow in (0, 1):
                ev(flow, i).wait_recv()

    def chip_at(dx, dz):
        return lax.rem(x + dx + NX, NX) * NZ + lax.rem(z + dz + NZ, NZ)

    start(0, 1, 2, 3)
    own_out = remote(feat, g.at[pl.ds(me * PER, PER)], ps.at[NX * NZ], pr.at[NX * NZ], partner)
    own_out.start()

    @pl.loop(1, NSPACE)
    def _(i):
        code_copy(i).start()
    own_code = pltpu.make_async_copy(codes.at[me], codes_in.at[me], ls.at[1])
    own_code.start()

    for a in range(3):
        for b in range(PER):
            at = pl.ds(pl.multiple_of(me * ROWS + b * BLOCK, BLOCK), BLOCK)
            posb[a, b] = jnp.broadcast_to(pos[a:a + 1, at], (BLOCK, BLOCK)).T
        at = pl.ds(pl.multiple_of(core * 512 + (chip // 4) * BLOCK, BLOCK), BLOCK)
        wt[a] = jnp.broadcast_to(wave[a:a + 1, at].astype(jnp.float32), (BLOCK, BLOCK)).T

    @pl.loop(0, NSPACE * PER // 8)
    def _(i):
        for j in range(8):
            at = pl.ds(pl.multiple_of(i * 1024 + j * BLOCK, BLOCK), BLOCK)
            posq[i * 8 + j] = pos[:, at]
    acc[...] = jnp.zeros_like(acc)
    s_acc[...] = jnp.zeros_like(s_acc)

    @pl.loop(0, PER)
    def _(b):
        at = pl.ds(pl.multiple_of(b * BLOCK, BLOCK), BLOCK)
        for h in range(NCORE):
            for part in range(2):
                k0 = h * 512 + part * 256
                t = None
                for a in range(3):
                    n = wave[a:a + 1, k0:k0 + 256].astype(jnp.float32)
                    p = posb[a, b]
                    term = jnp.concatenate([p, p], 1) * n
                    t = term if t is None else t + term
                c, s = cos_sin_turns(t * 0.125)
                col = h * 1024 + part * 256
                cs[at, col:col + 256] = c
                cs[at, col + 512:col + 768] = s

    mine = pl.ds(pl.multiple_of(lax.rem(chip, 4) * 32, 32), 32)
    nrow = [wt[a, mine, :] for a in range(3)]

    def distance(target, source):
        total = None
        there = posq[source]
        for a in range(3):
            off = jnp.abs(there[a:a + 1, :] - posb[a, target])
            off = jnp.minimum(off, 8.0 - off)
            total = off * off if total is None else total + off * off
        return jnp.sqrt(total) * SCALE

    def half_pair(target, source, f32_rows):
        es = expansion(distance(target, source))
        f = f32_rows.astype(jnp.bfloat16).reshape(8, 16, CH)
        total = None
        for k in range(0, NB, 4):
            lhs = jnp.concatenate(es[k:k + 4], 1)
            rhs = jnp.concatenate([(f * wb[k + j][None]).reshape(BLOCK, CH) for j in range(4)], 0)
            part = jnp.dot(lhs, rhs, preferred_element_type=jnp.float32)
            total = part if total is None else total + part
        return total

    def add_rows(targets, values):
        for b in range(PER):
            rows = acc[b * BLOCK:(b + 1) * BLOCK, :]
            for target, value in zip(targets, values):
                rows = rows + jnp.where(target == b, value, 0.0)
            acc[b * BLOCK:(b + 1) * BLOCK, :] = rows

    def chip_step(c):
        at = [pl.ds(pl.multiple_of(c * 1024 + i * BLOCK, BLOCK), BLOCK) for i in range(8)]
        blocks = []
        for i in range(8):
            t = nrow[0] * pos[0:1, at[i]] + nrow[1] * pos[1:2, at[i]] + nrow[2] * pos[2:3, at[i]]
            co, si = cos_sin_turns(t * 0.125)
            blocks.append(jnp.concatenate([co, si], 0))
        rows = g[pl.ds(c * NCORE * PER, NCORE * PER)].reshape(NCORE * ROWS, CH)
        s_acc[...] += jnp.dot(jnp.concatenate(blocks, 1), rows, preferred_element_type=jnp.float32)
        targets, values = [], []
        for h in range(NCORE):
            e = c * NCORE + h
            value = code_s[e, 0, 0]
            v = jnp.maximum(value - 1, 0)
            target = v // BLOCK
            source = lax.rem(v, BLOCK)
            local = jnp.where(value > 0, source - e * PER, -1)
            f = None
            for b in range(PER):
                block = g[e * PER + b].astype(jnp.float32)
                block = jnp.where(local == b, block, 0.0)
                f = block if f is None else f + block
            targets.append(target)
            values.append(half_pair(target, source, f))
        add_rows(targets, values)

    def both(c):
        to_partner(c).wait_recv()

    arrived(0, 1, 2, 3)
    start(4, 7, 5, 6, 8, 9, 14, 15)
    near = ((1, 0), (-1, 0), (0, 1), (0, -1))
    for dx, dz in near:
        to_partner(chip_at(dx, dz)).start()

    @pl.loop(1, NSPACE)
    def _(i):
        code_copy(i).wait_recv()
    own_code.wait()
    to_smem = pltpu.make_async_copy(codes_in, code_s, ls.at[2])
    to_smem.start()
    to_smem.wait()
    own.wait()
    own_out.wait_recv()
    arrived(4, 7)
    start(10, 11, 12, 13)
    chip_step(chip)

    def near_step(i):
        sign = 1 - 2 * lax.rem(i, 2)
        along = i // 2
        c = chip_at(sign * (1 - along), sign * along)
        both(c)
        chip_step(c)

    def diag_step(i):
        c = chip_at(1 - 2 * (i // 2), 1 - 2 * lax.rem(i, 2))
        both(c)
        chip_step(c)

    def far_step(i):
        c = chip_at(2 * (1 - i), 2 * i)
        both(c)
        chip_step(c)

    def knight_step(i):
        sign = 1 - 2 * lax.rem(i, 2)
        along = i // 2
        c = chip_at(2 * (1 - along) + sign * along, sign * (1 - along) + 2 * along)
        both(c)
        chip_step(c)

    pl.loop(0, 2)(near_step)
    arrived(5, 6, 8, 9)
    start(16, 17, 18, 19)
    for dx, dz in ((1, 1), (1, -1), (-1, 1), (-1, -1)):
        to_partner(chip_at(dx, dz)).start()
    pl.loop(2, 4)(near_step)
    arrived(10, 13)
    start(20, 21)
    arrived(14, 15)
    for dx, dz in ((2, 0), (0, 2)):
        to_partner(chip_at(dx, dz)).start()
    pl.loop(0, 4)(diag_step)
    arrived(11, 12, 16, 17, 18, 19)
    for dx, dz in ((2, 1), (2, -1), (1, 2), (-1, 2)):
        to_partner(chip_at(dx, dz)).start()
    pl.loop(0, 2)(far_step)
    arrived(20, 21)
    to_partner(chip_at(2, 2)).start()
    pl.loop(0, 4)(knight_step)
    both(chip_at(2, 2))
    chip_step(chip_at(2, 2))

    n = [r[:, 0:1] for r in nrow]
    q = (2.0 * math.pi / 8.0) ** 2 * (n[0] * n[0] + n[1] * n[1] + n[2] * n[2])
    sm = smear[...]
    kern = (4.0 * math.pi / q) * jnp.exp(-0.5 * q * (sm * sm))
    fg[core, 0, chip] = (s_acc[0:32, :] * kern).astype(jnp.bfloat16)
    fg[core, 1, chip] = (s_acc[32:64, :] * kern).astype(jnp.bfloat16)

    def f_copy(i):
        own_f = fg.at[core, :, chip]
        return remote(own_f, own_f, fs.at[i], fr.at[i], lax.rem(me + i, NSPACE))

    @pl.loop(1, NSPACE)
    def _(i):
        f_copy(i).start()

    @pl.loop(0, 8)
    def _(i):
        targets, values = [], []
        for h in range(2):
            s = 2 * i + h
            target, source = lax.rem(first[s], PER), second[s]
            f = g[source].astype(jnp.float32)
            f = jnp.where(s < count[0], f, 0.0)
            targets.append(target)
            values.append(half_pair(target, source, f))
        add_rows(targets, values)

    @pl.loop(1, NSPACE)
    def _(i):
        f_copy(i).wait_recv()

    def message(h):
        at = pl.ds(h * HALF, HALF)
        recip = jnp.dot(cs[at, :], fg[...].reshape(2 * KV, CH), preferred_element_type=jnp.float32)
        recip = recip * (4.0 / math.sqrt(16384.0 * KV))
        m[yme, at, :] = (0.25 * acc[at, :] + recip).astype(jnp.bfloat16)

    def hop(i, origin, rows, to):
        piece = m.at[origin, rows]
        return pltpu.make_async_remote_copy(
            src_ref=piece, dst_ref=piece, send_sem=ms.at[i], recv_sem=mr.at[i],
            device_id={"chan": to}, device_id_type=MESH)

    lo, hi = pl.ds(0, HALF), pl.ds(HALF, HALF)
    c0, c3 = hop(0, yme, lo, yup), hop(3, yme, lo, ydown)
    c1, c2 = hop(1, yme, hi, ydown), hop(2, yme, hi, yup)
    c4, c5 = hop(4, ydown, lo, yup), hop(5, yup, hi, ydown)
    message(0)
    c0.start()
    c3.start()
    message(1)
    c1.start()
    c2.start()

    def mixed(origin):
        rows = pl.ds(pl.multiple_of(origin * CH, CH), CH)
        return jnp.dot(m[origin], mix[rows, :], preferred_element_type=jnp.float32)

    total = feat[...].reshape(ROWS, CH).astype(jnp.float32) + mixed(yme)
    c0.wait_recv()
    c4.start()
    c1.wait_recv()
    c5.start()
    c2.wait_recv()
    total = total + mixed(ydown)
    c3.wait_recv()
    total = total + mixed(yup)
    c4.wait_recv()
    c5.wait_recv()
    out[...] = (total + mixed(yacross)).astype(jnp.bfloat16)

    for i in range(NEV):
        for flow in (0, 1):
            ev(flow, i).wait_send()
    own_out.wait_send()
    for c in (c0, c1, c2, c3, c4, c5):
        c.wait_send()

    @pl.loop(1, NSPACE)
    def _(i):
        code_copy(i).wait_send()
        f_copy(i).wait_send()

    @pl.loop(1, NX * NZ)
    def _(i):
        to_partner(lax.rem(chip + i, NX * NZ)).wait_send()


def body(features, positions, pair_first, pair_second, pair_counts, wave_index,
         radial_weight, smearing, mix_weight):
    dma = pltpu.SemaphoreType.DMA
    bf16, f32 = jnp.bfloat16, jnp.float32
    return pl.pallas_call(
        kernel,
        out_shape=jax.ShapeDtypeStruct((ROWS, CH), bf16),
        in_specs=[VM, SM, SM, SM] + [VM] * 8,
        out_specs=VM,
        scratch_shapes=[
            pltpu.VMEM((NSPACE * PER, BLOCK, CH), bf16),
            pltpu.VMEM((NSPACE, 1, BLOCK), jnp.int32),
            pltpu.VMEM((NSPACE, 1, BLOCK), jnp.int32),
            pltpu.SMEM((NSPACE, 1, BLOCK), jnp.int32),
            pltpu.VMEM((NCORE, 2, NX * NZ, 32, CH), bf16),
            pltpu.VMEM((ROWS, 2 * KV), bf16),
            pltpu.VMEM((ROWS, CH), f32),
            pltpu.VMEM((3, PER, BLOCK, BLOCK), f32),
            pltpu.VMEM((NSPACE * PER, 3, BLOCK), f32),
            pltpu.VMEM((3, BLOCK, BLOCK), f32),
            pltpu.VMEM((NB, 16, CH), bf16),
            pltpu.VMEM((64, CH), f32),
            pltpu.VMEM((NCHAN, ROWS, CH), bf16),
            dma((2, NEV)), dma((2, NEV)),
            dma((NSPACE,)), dma((NSPACE,)),
            dma((NX * NZ + 1,)), dma((NX * NZ + 1,)),
            dma((NSPACE,)), dma((NSPACE,)),
            dma((6,)), dma((6,)),
            dma((3,)),
        ],
        compiler_params=pltpu.CompilerParams(collective_id=0, has_side_effects=True),
        name="layer",
    )(features.reshape(PER, BLOCK, CH), pair_first, pair_second, pair_counts, pair_first[None, :], pair_second[None, :],
      pair_counts[None, :], positions, wave_index, radial_weight, smearing[None, :], mix_weight)


def solution(mesh):
    placed = (P("space", "chan"), P(), P("space"), P("space"), P("space"), P(),
              P(None, "chan"), P("chan"), P(None, "chan"))
    return jax.shard_map(
        body, mesh=mesh, in_specs=placed, out_specs=P("space", "chan"), check_vma=False
    )
```

profile of v0, /device:TPU:0, one launch (start us, length us, event | category | flops | bytes accessed | tf_op | source)
XLA Modules:
  0.0 57.9 jit_solution(10279111271117056665)
XLA Ops:
  0.7 55.7 %layer.1 = bf16[512,128]{1,0:T(8,128)(2,1)} custom-call(bf16[4,128,128]{2,1,0:T(8,128)(2,1)} %bitcast.6, s32[16]{0:T(128)} %first.1, s32[16]{0:T(128)} %second.1, s32[1]{0:T(128)} %copy.11.count, s32[1,16]{1,0:T(1,128)} %bitcast.7, s32[1,16]{1,0:T(1,128)} %bitcast.8, s32[1,1]{1,0:T(1,128)} %bitcast.5.count_v, f32[3,16384]{1,0:T(4,128)} %pos.1, ...), custom_call_target="tpu_custom_call" | custom-call | tf_op jit(solution)/shard_map/layer/pallas_call | solution.py:425
  56.3 1.6 %copy.12 = bf16[512,128]{1,0:T(8,128)(2,1)} copy(bf16[512,128]{1,0:T(8,128)(2,1)} %layer.1) | data formatting | bytes 262144
where the time goes:
time: 58 us; the launch traced here: 57.9 us
  Pallas kernels  55.7 us (96%)
  local copies, waits for them, and re-layouts  1.57 us (3%)
  between operations  0.66 us (1%)
    pallas_call x1, Pallas kernels, body(): pl.pallas_call(kernel, out_shape=jax.ShapeDtypeStruct((ROWS, CH), bf16),...  55.7 us
    unnamed x1, local copies, waits for them, and re-layouts  1.57 us

commit v1 on v0

--- a/solution.py
+++ b/solution.py
@@ -93,8 +93,8 @@
 
 
 def kernel(feat, first, second, count, first_v, second_v, count_v, pos, wave, weight, smear, mix, out,
-           g, codes, codes_in, code_s, fg, cs, acc, posb, posq, wt, wb, s_acc, m,
-           gs, gr, ks, kr, ps, pr, fs, fr, ms, mr, ls):
+           g, codes, codes_in, code_s, fg, cs, acc, posb, posq, wt, wb, part, parts, m,
+           gs, gr, ks, kr, ps, pr, rs, rr, fs, fr, ms, mr, ls):
     me = lax.axis_index("space")
     yme = lax.axis_index("chan")
     core = lax.rem(me, NCORE)
@@ -178,8 +178,9 @@
         for b in range(PER):
             at = pl.ds(pl.multiple_of(me * ROWS + b * BLOCK, BLOCK), BLOCK)
             posb[a, b] = jnp.broadcast_to(pos[a:a + 1, at], (BLOCK, BLOCK)).T
-        at = pl.ds(pl.multiple_of(core * 512 + (chip // 4) * BLOCK, BLOCK), BLOCK)
-        wt[a] = jnp.broadcast_to(wave[a:a + 1, at].astype(jnp.float32), (BLOCK, BLOCK)).T
+        for b in range(KV // BLOCK):
+            n = wave[a:a + 1, b * BLOCK:(b + 1) * BLOCK].astype(jnp.float32)
+            wt[a, b * BLOCK:(b + 1) * BLOCK, :] = jnp.broadcast_to(n, (BLOCK, BLOCK)).T
 
     @pl.loop(0, NSPACE * PER // 8)
     def _(i):
@@ -187,7 +188,43 @@
             at = pl.ds(pl.multiple_of(i * 1024 + j * BLOCK, BLOCK), BLOCK)
             posq[i * 8 + j] = pos[:, at]
     acc[...] = jnp.zeros_like(acc)
-    s_acc[...] = jnp.zeros_like(s_acc)
+
+    @pl.loop(0, NX * NZ)
+    def _(c):
+        rows = []
+        for h in range(NCORE):
+            ks_at = pl.ds(pl.multiple_of(h * 512 + c * 32, 32), 32)
+            n = [wt[a, ks_at, :] for a in range(3)]
+            cols = []
+            for b in range(PER):
+                at = pl.ds(pl.multiple_of(me * ROWS + b * BLOCK, BLOCK), BLOCK)
+                t = n[0] * pos[0:1, at] + n[1] * pos[1:2, at] + n[2] * pos[2:3, at]
+                co, si = cos_sin_turns(t * 0.125)
+                cols.append(jnp.concatenate([co, si], 0))
+            rows.append(jnp.concatenate(cols, 1))
+        both_parts = jnp.dot(jnp.concatenate(rows, 0), feat[...].reshape(ROWS, CH),
+                             preferred_element_type=jnp.float32).astype(jnp.bfloat16)
+        part[c * NCORE] = both_parts[0:64]
+        part[c * NCORE + 1] = both_parts[64:128]
+
+    parts[me] = part[me]
+
+    def part_copy(i):
+        to = lax.rem(me + i, NSPACE)
+        return remote(part.at[to], parts.at[me], rs.at[i], rr.at[i], to)
+
+    arrived(0, 1)
+    start(4, 5, 6, 7, 8, 9)
+
+    @pl.loop(1, NSPACE)
+    def _(i):
+        part_copy(i).start()
+
+    arrived(2, 3)
+    start(14, 15)
+    near = ((1, 0), (-1, 0), (0, 1), (0, -1))
+    for dx, dz in near:
+        to_partner(chip_at(dx, dz)).start()
 
     @pl.loop(0, PER)
     def _(b):
@@ -206,9 +243,6 @@
                 cs[at, col:col + 256] = c
                 cs[at, col + 512:col + 768] = s
 
-    mine = pl.ds(pl.multiple_of(lax.rem(chip, 4) * 32, 32), 32)
-    nrow = [wt[a, mine, :] for a in range(3)]
-
     def distance(target, source):
         total = None
         there = posq[source]
@@ -237,14 +271,6 @@
             acc[b * BLOCK:(b + 1) * BLOCK, :] = rows
 
     def chip_step(c):
-        at = [pl.ds(pl.multiple_of(c * 1024 + i * BLOCK, BLOCK), BLOCK) for i in range(8)]
-        blocks = []
-        for i in range(8):
-            t = nrow[0] * pos[0:1, at[i]] + nrow[1] * pos[1:2, at[i]] + nrow[2] * pos[2:3, at[i]]
-            co, si = cos_sin_turns(t * 0.125)
-            blocks.append(jnp.concatenate([co, si], 0))
-        rows = g[pl.ds(c * NCORE * PER, NCORE * PER)].reshape(NCORE * ROWS, CH)
-        s_acc[...] += jnp.dot(jnp.concatenate(blocks, 1), rows, preferred_element_type=jnp.float32)
         targets, values = [], []
         for h in range(NCORE):
             e = c * NCORE + h
@@ -265,10 +291,11 @@
     def both(c):
         to_partner(c).wait_recv()
 
-    arrived(0, 1, 2, 3)
-    start(4, 7, 5, 6, 8, 9, 14, 15)
-    near = ((1, 0), (-1, 0), (0, 1), (0, -1))
-    for dx, dz in near:
+    arrived(4, 7)
+    start(10, 11, 12, 13)
+    arrived(5, 6, 8, 9)
+    start(16, 17, 18, 19)
+    for dx, dz in ((1, 1), (1, -1), (-1, 1), (-1, -1)):
         to_partner(chip_at(dx, dz)).start()
 
     @pl.loop(1, NSPACE)
@@ -280,8 +307,6 @@
     to_smem.wait()
     own.wait()
     own_out.wait_recv()
-    arrived(4, 7)
-    start(10, 11, 12, 13)
     chip_step(chip)
 
     def near_step(i):
@@ -309,41 +334,55 @@
         chip_step(c)
 
     pl.loop(0, 2)(near_step)
-    arrived(5, 6, 8, 9)
-    start(16, 17, 18, 19)
-    for dx, dz in ((1, 1), (1, -1), (-1, 1), (-1, -1)):
-        to_partner(chip_at(dx, dz)).start()
-    pl.loop(2, 4)(near_step)
     arrived(10, 13)
     start(20, 21)
     arrived(14, 15)
     for dx, dz in ((2, 0), (0, 2)):
         to_partner(chip_at(dx, dz)).start()
-    pl.loop(0, 4)(diag_step)
+    pl.loop(2, 4)(near_step)
+
+    @pl.loop(1, NSPACE)
+    def _(i):
+        part_copy(i).wait_recv()
+    total = parts[0].astype(jnp.float32)
+    for j in range(1, NSPACE):
+        total = total + parts[j].astype(jnp.float32)
+    mine = pl.ds(pl.multiple_of(core * 512 + chip * 32, 32), 32)
+    n = [wt[a, mine, 0:1] for a in range(3)]
+    q = (2.0 * math.pi / 8.0) ** 2 * (n[0] * n[0] + n[1] * n[1] + n[2] * n[2])
+    sm = smear[...]
+    kern = (4.0 * math.pi / q) * jnp.exp(-0.5 * q * (sm * sm))
+    fg[core, 0, chip] = (total[0:32, :] * kern).astype(jnp.bfloat16)
+    fg[core, 1, chip] = (total[32:64, :] * kern).astype(jnp.bfloat16)
+
+    def f_copy(i):
+        own_f = fg.at[core, :, chip]
+        return remote(own_f, own_f, fs.at[i], fr.at[i], lax.rem(me + i, NSPACE))
+
+    @pl.loop(1, NSPACE)
+    def _(i):
+        f_copy(i).start()
+
+    pl.loop(0, 2)(diag_step)
     arrived(11, 12, 16, 17, 18, 19)
     for dx, dz in ((2, 1), (2, -1), (1, 2), (-1, 2)):
         to_partner(chip_at(dx, dz)).start()
-    pl.loop(0, 2)(far_step)
     arrived(20, 21)
     to_partner(chip_at(2, 2)).start()
+    pl.loop(2, 4)(diag_step)
+    pl.loop(0, 2)(far_step)
     pl.loop(0, 4)(knight_step)
     both(chip_at(2, 2))
     chip_step(chip_at(2, 2))
 
-    n = [r[:, 0:1] for r in nrow]
-    q = (2.0 * math.pi / 8.0) ** 2 * (n[0] * n[0] + n[1] * n[1] + n[2] * n[2])
-    sm = smear[...]
-    kern = (4.0 * math.pi / q) * jnp.exp(-0.5 * q * (sm * sm))
-    fg[core, 0, chip] = (s_acc[0:32, :] * kern).astype(jnp.bfloat16)
-    fg[core, 1, chip] = (s_acc[32:64, :] * kern).astype(jnp.bfloat16)
-
-    def f_copy(i):
-        own_f = fg.at[core, :, chip]
-        return remote(own_f, own_f, fs.at[i], fr.at[i], lax.rem(me + i, NSPACE))
-
-    @pl.loop(1, NSPACE)
-    def _(i):
-        f_copy(i).start()
+    @pl.loop(1, NSPACE)
+    def _(i):
+        f_copy(i).wait_recv()
+
+    for b in range(PER):
+        at = pl.ds(b * BLOCK, BLOCK)
+        recip = jnp.dot(cs[at, :], fg[...].reshape(2 * KV, CH), preferred_element_type=jnp.float32)
+        acc[at, :] += recip * (4.0 * 4.0 / math.sqrt(16384.0 * KV))
 
     @pl.loop(0, 8)
     def _(i):
@@ -357,15 +396,9 @@
             values.append(half_pair(target, source, f))
         add_rows(targets, values)
 
-    @pl.loop(1, NSPACE)
-    def _(i):
-        f_copy(i).wait_recv()
-
     def message(h):
         at = pl.ds(h * HALF, HALF)
-        recip = jnp.dot(cs[at, :], fg[...].reshape(2 * KV, CH), preferred_element_type=jnp.float32)
-        recip = recip * (4.0 / math.sqrt(16384.0 * KV))
-        m[yme, at, :] = (0.25 * acc[at, :] + recip).astype(jnp.bfloat16)
+        m[yme, at, :] = (0.25 * acc[at, :]).astype(jnp.bfloat16)
 
     def hop(i, origin, rows, to):
         piece = m.at[origin, rows]
@@ -411,6 +444,7 @@
     @pl.loop(1, NSPACE)
     def _(i):
         code_copy(i).wait_send()
+        part_copy(i).wait_send()
         f_copy(i).wait_send()
 
     @pl.loop(1, NX * NZ)
@@ -437,13 +471,15 @@
             pltpu.VMEM((ROWS, CH), f32),
             pltpu.VMEM((3, PER, BLOCK, BLOCK), f32),
             pltpu.VMEM((NSPACE * PER, 3, BLOCK), f32),
-            pltpu.VMEM((3, BLOCK, BLOCK), f32),
+            pltpu.VMEM((3, KV, BLOCK), f32),
             pltpu.VMEM((NB, 16, CH), bf16),
-            pltpu.VMEM((64, CH), f32),
+            pltpu.VMEM((NSPACE, 64, CH), bf16),
+            pltpu.VMEM((NSPACE, 64, CH), bf16),
             pltpu.VMEM((NCHAN, ROWS, CH), bf16),
             dma((2, NEV)), dma((2, NEV)),
             dma((NSPACE,)), dma((NSPACE,)),
             dma((NX * NZ + 1,)), dma((NX * NZ + 1,)),
+            dma((NSPACE,)), dma((NSPACE,)),
             dma((NSPACE,)), dma((NSPACE,)),
             dma((6,)), dma((6,)),
             dma((3,)),

time: 58 us -> 66.6 us (1.15)
  the two profiles are of different devices: /device:TPU:0 before, /device:TPU:2 now
where the time goes in v1:
time: 66.6 us; the launch traced here: 66.5 us
  Pallas kernels  64.2 us (96%)
  local copies, waits for them, and re-layouts  1.57 us (2%)
    pallas_call x1, Pallas kernels, body(): pl.pallas_call(kernel, out_shape=jax.ShapeDtypeStruct((ROWS, CH), bf16),...  64.2 us
    unnamed x1, local copies, waits for them, and re-layouts  1.57 us

profile of v1, /device:TPU:2, one launch (start us, length us, event | category | flops | bytes accessed | tf_op | source)
XLA Modules:
  0.0 66.5 jit_solution(13541509119932172696)
XLA Ops:
  0.7 64.2 %layer.1 = bf16[512,128]{1,0:T(8,128)(2,1)} custom-call(bf16[4,128,128]{2,1,0:T(8,128)(2,1)} %bitcast.6, s32[16]{0:T(128)} %first.1, s32[16]{0:T(128)} %second.1, s32[1]{0:T(128)} %copy.11.count, s32[1,16]{1,0:T(1,128)} %bitcast.7, s32[1,16]{1,0:T(1,128)} %bitcast.8, s32[1,1]{1,0:T(1,128)} %bitcast.5.count_v, f32[3,16384]{1,0:T(4,128)} %pos.1, ...), custom_call_target="tpu_custom_call" | custom-call | tf_op jit(solution)/shard_map/layer/pallas_call | solution.py:459
  64.9 1.6 %copy.12 = bf16[512,128]{1,0:T(8,128)(2,1)} copy(bf16[512,128]{1,0:T(8,128)(2,1)} %layer.1) | data formatting | bytes 262144

commit v2 on v0

--- a/solution.py
+++ b/solution.py
@@ -222,9 +222,9 @@
         es = expansion(distance(target, source))
         f = f32_rows.astype(jnp.bfloat16).reshape(8, 16, CH)
         total = None
-        for k in range(0, NB, 4):
-            lhs = jnp.concatenate(es[k:k + 4], 1)
-            rhs = jnp.concatenate([(f * wb[k + j][None]).reshape(BLOCK, CH) for j in range(4)], 0)
+        for k in range(0, NB, 2):
+            lhs = jnp.concatenate(es[k:k + 2], 1)
+            rhs = jnp.concatenate([(f * wb[k + j][None]).reshape(BLOCK, CH) for j in range(2)], 0)
             part = jnp.dot(lhs, rhs, preferred_element_type=jnp.float32)
             total = part if total is None else total + part
         return total
@@ -236,7 +236,7 @@
                 rows = rows + jnp.where(target == b, value, 0.0)
             acc[b * BLOCK:(b + 1) * BLOCK, :] = rows
 
-    def chip_step(c):
+    def add_factors(c):
         at = [pl.ds(pl.multiple_of(c * 1024 + i * BLOCK, BLOCK), BLOCK) for i in range(8)]
         blocks = []
         for i in range(8):
@@ -245,31 +245,70 @@
             blocks.append(jnp.concatenate([co, si], 0))
         rows = g[pl.ds(c * NCORE * PER, NCORE * PER)].reshape(NCORE * ROWS, CH)
         s_acc[...] += jnp.dot(jnp.concatenate(blocks, 1), rows, preferred_element_type=jnp.float32)
-        targets, values = [], []
-        for h in range(NCORE):
-            e = c * NCORE + h
-            value = code_s[e, 0, 0]
-            v = jnp.maximum(value - 1, 0)
-            target = v // BLOCK
-            source = lax.rem(v, BLOCK)
-            local = jnp.where(value > 0, source - e * PER, -1)
-            f = None
-            for b in range(PER):
-                block = g[e * PER + b].astype(jnp.float32)
-                block = jnp.where(local == b, block, 0.0)
-                f = block if f is None else f + block
-            targets.append(target)
-            values.append(half_pair(target, source, f))
-        add_rows(targets, values)
+
+    def slot_of(e):
+        value = code_s[e, 0, 0]
+        v = jnp.maximum(value - 1, 0)
+        return value, v // BLOCK, lax.rem(v, BLOCK)
+
+    def own_slot(s):
+        f = g[second[s]].astype(jnp.float32)
+        return lax.rem(first[s], PER), second[s], jnp.where(s < count[0], f, 0.0)
+
+    def chosen_block(e):
+        value, target, source = slot_of(e)
+        local = jnp.where(value > 0, source - e * PER, -1)
+        f = None
+        for b in range(PER):
+            block = jnp.where(local == b, g[e * PER + b].astype(jnp.float32), 0.0)
+            f = block if f is None else f + block
+        return target, source, f
+
+    def loaded_block(e):
+        value, target, source = slot_of(e)
+        return target, source, jnp.where(value > 0, g[source].astype(jnp.float32), 0.0)
+
+    def add_pairs(items):
+        add_rows([t for t, _, _ in items], [half_pair(*item) for item in items])
+
+    def early(*chips):
+        add_pairs([chosen_block(c * NCORE + h) for c in chips for h in range(NCORE)])
 
     def both(c):
         to_partner(c).wait_recv()
 
-    arrived(0, 1, 2, 3)
-    start(4, 7, 5, 6, 8, 9, 14, 15)
     near = ((1, 0), (-1, 0), (0, 1), (0, -1))
-    for dx, dz in near:
-        to_partner(chip_at(dx, dz)).start()
+    diag = ((1, 1), (1, -1), (-1, 1), (-1, -1))
+    far = ((2, 0), (0, 2))
+    knight = ((2, 1), (2, -1), (1, 2), (-1, 2))
+
+    def forward(group):
+        for dx, dz in group:
+            to_partner(chip_at(dx, dz)).start()
+
+    def near_factors(i):
+        sign, along = 1 - 2 * lax.rem(i, 2), i // 2
+        c = chip_at(sign * (1 - along), sign * along)
+        both(c)
+        add_factors(c)
+
+    def diag_factors(i):
+        c = chip_at(1 - 2 * (i // 2), 1 - 2 * lax.rem(i, 2))
+        both(c)
+        add_factors(c)
+
+    def two_factors(i):
+        late = i // 4
+        add_factors(chip_at(2 * (1 - late) + late * ((i - 4) + (i - 4) // 2), (1 - late) * i + 2 * late))
+
+    arrived(0, 1)
+    start(4, 5, 6, 7, 8, 9)
+    arrived(2, 3)
+    start(14, 15)
+    forward(near)
+    own.wait()
+    own_out.wait_recv()
+    add_factors(chip)
 
     @pl.loop(1, NSPACE)
     def _(i):
@@ -278,57 +317,31 @@
     to_smem = pltpu.make_async_copy(codes_in, code_s, ls.at[2])
     to_smem.start()
     to_smem.wait()
-    own.wait()
-    own_out.wait_recv()
+    pl.loop(0, 4)(near_factors)
     arrived(4, 7)
     start(10, 11, 12, 13)
-    chip_step(chip)
-
-    def near_step(i):
-        sign = 1 - 2 * lax.rem(i, 2)
-        along = i // 2
-        c = chip_at(sign * (1 - along), sign * along)
-        both(c)
-        chip_step(c)
-
-    def diag_step(i):
-        c = chip_at(1 - 2 * (i // 2), 1 - 2 * lax.rem(i, 2))
-        both(c)
-        chip_step(c)
-
-    def far_step(i):
-        c = chip_at(2 * (1 - i), 2 * i)
-        both(c)
-        chip_step(c)
-
-    def knight_step(i):
-        sign = 1 - 2 * lax.rem(i, 2)
-        along = i // 2
-        c = chip_at(2 * (1 - along) + sign * along, sign * (1 - along) + 2 * along)
-        both(c)
-        chip_step(c)
-
-    pl.loop(0, 2)(near_step)
+    early(chip, chip_at(1, 0))
     arrived(5, 6, 8, 9)
     start(16, 17, 18, 19)
-    for dx, dz in ((1, 1), (1, -1), (-1, 1), (-1, -1)):
-        to_partner(chip_at(dx, dz)).start()
-    pl.loop(2, 4)(near_step)
+    forward(diag)
+    arrived(14, 15)
+    forward(far)
+    early(chip_at(-1, 0), chip_at(0, 1))
     arrived(10, 13)
     start(20, 21)
-    arrived(14, 15)
-    for dx, dz in ((2, 0), (0, 2)):
-        to_partner(chip_at(dx, dz)).start()
-    pl.loop(0, 4)(diag_step)
+    pl.loop(0, 4)(diag_factors)
+    early(chip_at(0, -1), chip_at(1, 1))
     arrived(11, 12, 16, 17, 18, 19)
-    for dx, dz in ((2, 1), (2, -1), (1, 2), (-1, 2)):
-        to_partner(chip_at(dx, dz)).start()
-    pl.loop(0, 2)(far_step)
+    forward(knight)
+    early(chip_at(1, -1), chip_at(-1, 1))
     arrived(20, 21)
-    to_partner(chip_at(2, 2)).start()
-    pl.loop(0, 4)(knight_step)
-    both(chip_at(2, 2))
-    chip_step(chip_at(2, 2))
+    forward(((2, 2),))
+    for dx, dz in far:
+        both(chip_at(dx, dz))
+    early(chip_at(2, 0), chip_at(0, 2))
+    for dx, dz in knight + ((2, 2),):
+        both(chip_at(dx, dz))
+    pl.loop(0, 7)(two_factors)
 
     n = [r[:, 0:1] for r in nrow]
     q = (2.0 * math.pi / 8.0) ** 2 * (n[0] * n[0] + n[1] * n[1] + n[2] * n[2])
@@ -345,17 +358,13 @@
     def _(i):
         f_copy(i).start()
 
-    @pl.loop(0, 8)
-    def _(i):
-        targets, values = [], []
-        for h in range(2):
-            s = 2 * i + h
-            target, source = lax.rem(first[s], PER), second[s]
-            f = g[source].astype(jnp.float32)
-            f = jnp.where(s < count[0], f, 0.0)
-            targets.append(target)
-            values.append(half_pair(target, source, f))
-        add_rows(targets, values)
+    @pl.loop(0, 6)
+    def _(i):
+        late, last = i // 3, i // 5
+        c = chip_at(2 * (1 - late) + late * (1 + 2 * (i - 3) - 2 * last), (1 - late) * (1 + i) + late * (2 + last))
+        add_pairs([loaded_block(c * NCORE), loaded_block(c * NCORE + 1), own_slot(2 * i), own_slot(2 * i + 1)])
+
+    add_pairs([own_slot(s) for s in range(12, 16)])
 
     @pl.loop(1, NSPACE)
     def _(i):

time: 58 us -> 56.7 us (0.978)
  Pallas kernels: 55.7 us -> 54.4 us
    pallas_call x1, Pallas kernels: 55.7 us -> 54.4 us  [body(): pl.pallas_call(kernel, out_shape=jax.ShapeDtypeStruct((ROWS, CH), bf16),...]
where the time goes in v2:
time: 56.7 us; the launch traced here: 56.6 us
  Pallas kernels  54.4 us (96%)
  local copies, waits for them, and re-layouts  1.57 us (3%)
  between operations  0.66 us (1%)
    pallas_call x1, Pallas kernels, body(): pl.pallas_call(kernel, out_shape=jax.ShapeDtypeStruct((ROWS, CH), bf16),...  54.4 us
    unnamed x1, local copies, waits for them, and re-layouts  1.57 us

profile of v2, /device:TPU:0, one launch (start us, length us, event | category | flops | bytes accessed | tf_op | source)
XLA Modules:
  0.0 56.6 jit_solution(16965378655761746881)
XLA Ops:
  0.7 54.4 %layer.1 = bf16[512,128]{1,0:T(8,128)(2,1)} custom-call(bf16[4,128,128]{2,1,0:T(8,128)(2,1)} %bitcast.6, s32[16]{0:T(128)} %first.1, s32[16]{0:T(128)} %second.1, s32[1]{0:T(128)} %copy.11.count, s32[1,16]{1,0:T(1,128)} %bitcast.7, s32[1,16]{1,0:T(1,128)} %bitcast.8, s32[1,1]{1,0:T(1,128)} %bitcast.5.count_v, f32[3,16384]{1,0:T(4,128)} %pos.1, ...), custom_call_target="tpu_custom_call" | custom-call | tf_op jit(solution)/shard_map/layer/pallas_call | solution.py:434
  55.0 1.6 %copy.12 = bf16[512,128]{1,0:T(8,128)(2,1)} copy(bf16[512,128]{1,0:T(8,128)(2,1)} %layer.1) | data formatting | bytes 262144

commit v3 on v2

--- a/solution.py
+++ b/solution.py
@@ -297,18 +297,25 @@
         both(c)
         add_factors(c)
 
-    def two_factors(i):
-        late = i // 4
-        add_factors(chip_at(2 * (1 - late) + late * ((i - 4) + (i - 4) // 2), (1 - late) * i + 2 * late))
-
+    def far_factors(i):
+        c = chip_at(2 * (1 - i), 2 * i)
+        both(c)
+        add_factors(c)
+
+    def knight_factors(i):
+        sign, along = 1 - 2 * lax.rem(i, 2), i // 2
+        c = chip_at(2 * (1 - along) + sign * along, sign * (1 - along) + 2 * along)
+        both(c)
+        add_factors(c)
+
+    own.wait()
+    own_out.wait_recv()
+    add_factors(chip)
     arrived(0, 1)
     start(4, 5, 6, 7, 8, 9)
     arrived(2, 3)
     start(14, 15)
     forward(near)
-    own.wait()
-    own_out.wait_recv()
-    add_factors(chip)
 
     @pl.loop(1, NSPACE)
     def _(i):
@@ -317,31 +324,29 @@
     to_smem = pltpu.make_async_copy(codes_in, code_s, ls.at[2])
     to_smem.start()
     to_smem.wait()
-    pl.loop(0, 4)(near_factors)
     arrived(4, 7)
     start(10, 11, 12, 13)
-    early(chip, chip_at(1, 0))
+    pl.loop(0, 4)(near_factors)
     arrived(5, 6, 8, 9)
     start(16, 17, 18, 19)
     forward(diag)
     arrived(14, 15)
     forward(far)
-    early(chip_at(-1, 0), chip_at(0, 1))
+    early(chip, chip_at(1, 0))
     arrived(10, 13)
     start(20, 21)
-    pl.loop(0, 4)(diag_factors)
-    early(chip_at(0, -1), chip_at(1, 1))
+    early(chip_at(-1, 0), chip_at(0, 1))
     arrived(11, 12, 16, 17, 18, 19)
     forward(knight)
-    early(chip_at(1, -1), chip_at(-1, 1))
+    pl.loop(0, 4)(diag_factors)
+    pl.loop(0, 2)(far_factors)
+    early(chip_at(0, -1), chip_at(1, 1))
     arrived(20, 21)
     forward(((2, 2),))
-    for dx, dz in far:
-        both(chip_at(dx, dz))
-    early(chip_at(2, 0), chip_at(0, 2))
-    for dx, dz in knight + ((2, 2),):
-        both(chip_at(dx, dz))
-    pl.loop(0, 7)(two_factors)
+    pl.loop(0, 4)(knight_factors)
+    early(chip_at(1, -1), chip_at(-1, 1))
+    both(chip_at(2, 2))
+    add_factors(chip_at(2, 2))
 
     n = [r[:, 0:1] for r in nrow]
     q = (2.0 * math.pi / 8.0) ** 2 * (n[0] * n[0] + n[1] * n[1] + n[2] * n[2])
@@ -358,63 +363,73 @@
     def _(i):
         f_copy(i).start()
 
-    @pl.loop(0, 6)
-    def _(i):
-        late, last = i // 3, i // 5
-        c = chip_at(2 * (1 - late) + late * (1 + 2 * (i - 3) - 2 * last), (1 - late) * (1 + i) + late * (2 + last))
+    @pl.loop(0, 8)
+    def _(i):
+        late, last = i // 4, i // 7
+        dx = 2 * (1 - late) + late * ((i - 4) + (i - 4) // 2 - last)
+        c = chip_at(dx, (1 - late) * i + late * (2 + last))
         add_pairs([loaded_block(c * NCORE), loaded_block(c * NCORE + 1), own_slot(2 * i), own_slot(2 * i + 1)])
 
-    add_pairs([own_slot(s) for s in range(12, 16)])
-
     @pl.loop(1, NSPACE)
     def _(i):
         f_copy(i).wait_recv()
 
-    def message(h):
-        at = pl.ds(h * HALF, HALF)
+    def message(b):
+        at = pl.ds(b * BLOCK, BLOCK)
         recip = jnp.dot(cs[at, :], fg[...].reshape(2 * KV, CH), preferred_element_type=jnp.float32)
         recip = recip * (4.0 / math.sqrt(16384.0 * KV))
-        m[yme, at, :] = (0.25 * acc[at, :] + recip).astype(jnp.bfloat16)
-
-    def hop(i, origin, rows, to):
-        piece = m.at[origin, rows]
+        m[yme, b] = (0.25 * acc[at, :] + recip).astype(jnp.bfloat16)
+
+    def hop(i, origin, b, to):
+        piece = m.at[origin, b]
         return pltpu.make_async_remote_copy(
             src_ref=piece, dst_ref=piece, send_sem=ms.at[i], recv_sem=mr.at[i],
             device_id={"chan": to}, device_id_type=MESH)
 
-    lo, hi = pl.ds(0, HALF), pl.ds(HALF, HALF)
-    c0, c3 = hop(0, yme, lo, yup), hop(3, yme, lo, ydown)
-    c1, c2 = hop(1, yme, hi, ydown), hop(2, yme, hi, yup)
-    c4, c5 = hop(4, ydown, lo, yup), hop(5, yup, hi, ydown)
+    ups = [hop(b, yme, b, yup) for b in range(PER)]
+    downs = [hop(PER + b, yme, b, ydown) for b in range(PER)]
+    relays = [hop(2 * PER + b, ydown, b, yup) for b in (0, 1)] + [hop(2 * PER + b, yup, b, ydown) for b in (2, 3)]
     message(0)
-    c0.start()
-    c3.start()
+    message(2)
+    ups[0].start()
+    downs[2].start()
     message(1)
-    c1.start()
-    c2.start()
+    message(3)
+    ups[1].start()
+    downs[3].start()
+    ups[2].start()
+    downs[0].start()
+    ups[3].start()
+    downs[1].start()
 
     def mixed(origin):
         rows = pl.ds(pl.multiple_of(origin * CH, CH), CH)
-        return jnp.dot(m[origin], mix[rows, :], preferred_element_type=jnp.float32)
-
+        return jnp.dot(m[origin].reshape(ROWS, CH), mix[rows, :], preferred_element_type=jnp.float32)
+
+    ups[0].wait_recv()
+    relays[0].start()
+    downs[2].wait_recv()
+    relays[2].start()
+    ups[1].wait_recv()
+    relays[1].start()
+    downs[3].wait_recv()
+    relays[3].start()
     total = feat[...].reshape(ROWS, CH).astype(jnp.float32) + mixed(yme)
-    c0.wait_recv()
-    c4.start()
-    c1.wait_recv()
-    c5.start()
-    c2.wait_recv()
+    ups[2].wait_recv()
+    ups[3].wait_recv()
     total = total + mixed(ydown)
-    c3.wait_recv()
+    downs[0].wait_recv()
+    downs[1].wait_recv()
     total = total + mixed(yup)
-    c4.wait_recv()
-    c5.wait_recv()
+    for c in relays:
+        c.wait_recv()
     out[...] = (total + mixed(yacross)).astype(jnp.bfloat16)
 
     for i in range(NEV):
         for flow in (0, 1):
             ev(flow, i).wait_send()
     own_out.wait_send()
-    for c in (c0, c1, c2, c3, c4, c5):
+    for c in ups + downs + relays:
         c.wait_send()
 
     @pl.loop(1, NSPACE)
@@ -449,12 +464,12 @@
             pltpu.VMEM((3, BLOCK, BLOCK), f32),
             pltpu.VMEM((NB, 16, CH), bf16),
             pltpu.VMEM((64, CH), f32),
-            pltpu.VMEM((NCHAN, ROWS, CH), bf16),
+            pltpu.VMEM((NCHAN, PER, BLOCK, CH), bf16),
             dma((2, NEV)), dma((2, NEV)),
             dma((NSPACE,)), dma((NSPACE,)),
             dma((NX * NZ + 1,)), dma((NX * NZ + 1,)),
             dma((NSPACE,)), dma((NSPACE,)),
-            dma((6,)), dma((6,)),
+            dma((3 * PER,)), dma((3 * PER,)),
             dma((3,)),
         ],
         compiler_params=pltpu.CompilerParams(collective_id=0, has_side_effects=True),

time: 56.7 us -> 57.7 us (1.018)
  Pallas kernels: 54.4 us -> 55.4 us
    pallas_call x1, Pallas kernels: 54.4 us -> 55.4 us  [body(): pl.pallas_call(kernel, out_shape=jax.ShapeDtypeStruct((ROWS, CH), bf16),...]
where the time goes in v3:
time: 57.7 us; the launch traced here: 57.6 us
  Pallas kernels  55.4 us (96%)
  local copies, waits for them, and re-layouts  1.57 us (3%)
  between operations  0.66 us (1%)
    pallas_call x1, Pallas kernels, body(): pl.pallas_call(kernel, out_shape=jax.ShapeDtypeStruct((ROWS, CH), bf16),...  55.4 us
    unnamed x1, local copies, waits for them, and re-layouts  1.57 us

profile of v3, /device:TPU:0, one launch (start us, length us, event | category | flops | bytes accessed | tf_op | source)
XLA Modules:
  0.0 57.6 jit_solution(6045410482414709207)
XLA Ops:
  0.7 55.4 %layer.1 = bf16[512,128]{1,0:T(8,128)(2,1)} custom-call(bf16[4,128,128]{2,1,0:T(8,128)(2,1)} %bitcast.6, s32[16]{0:T(128)} %first.1, s32[16]{0:T(128)} %second.1, s32[1]{0:T(128)} %copy.11.count, s32[1,16]{1,0:T(1,128)} %bitcast.7, s32[1,16]{1,0:T(1,128)} %bitcast.8, s32[1,1]{1,0:T(1,128)} %bitcast.5.count_v, f32[3,16384]{1,0:T(4,128)} %pos.1, ...), custom_call_target="tpu_custom_call" | custom-call | tf_op jit(solution)/shard_map/layer/pallas_call | solution.py:449
  56.0 1.6 %copy.12 = bf16[512,128]{1,0:T(8,128)(2,1)} copy(bf16[512,128]{1,0:T(8,128)(2,1)} %layer.1) | data formatting | bytes 262144

commit v4 on v3

--- a/solution.py
+++ b/solution.py
@@ -73,13 +73,16 @@
 NEV = len(EVENTS)
 
 
-def expansion(d):
+def expansion(d2):
     out = [None] * NB
     half = GROUP // 2
+    shrink = 1.0 / (4.0 * DELTA * DELTA)
+    dk = d2 * shrink
     for c in range(half, NB, GROUP):
-        a, b = d - c * DELTA, c * DELTA - d
-        mid = jnp.exp2(a * b)
-        up, down = jnp.exp2(a * (2.0 * DELTA)), jnp.exp2(b * (2.0 * DELTA))
+        centre = 2.0 * c * DELTA * DELTA
+        a = d2 - centre
+        mid = jnp.exp2(a * (centre * shrink - dk))
+        up, down = jnp.exp2(a), jnp.exp2(centre - d2)
         out[c] = mid
         e = mid
         for j in range(1, GROUP - half):
@@ -93,7 +96,7 @@
 
 
 def kernel(feat, first, second, count, first_v, second_v, count_v, pos, wave, weight, smear, mix, out,
-           g, codes, codes_in, code_s, fg, cs, acc, posb, posq, wt, wb, s_acc, m,
+           g, table, codes, code_s, fg, cs, acc, posb, posq, wt, wb, s_acc, m,
            gs, gr, ks, kr, ps, pr, fs, fr, ms, mr, ls):
     me = lax.axis_index("space")
     yme = lax.axis_index("chan")
@@ -106,31 +109,27 @@
 
     barrier = pltpu.get_barrier_semaphore()
 
-    @pl.loop(1, NSPACE)
-    def _(i):
-        pl.semaphore_signal(barrier, inc=1, device_id={"space": lax.rem(me + i, NSPACE)},
-                            device_id_type=MESH)
+    xpeers = [place(x + i, z, core) for i in (1, 2, 3)]
+    zpeers = [place(x, z + i, core) for i in (1, 2, 3)]
+    for peer in xpeers + zpeers + [partner]:
+        pl.semaphore_signal(barrier, inc=1, device_id={"space": peer}, device_id_type=MESH)
     for peer in (yup, ydown):
         pl.semaphore_signal(barrier, inc=1, device_id={"chan": peer}, device_id_type=MESH)
 
     own = pltpu.make_async_copy(feat, g.at[pl.ds(me * PER, PER)], ls.at[0])
     own.start()
 
-    sec = second_v[...]
-    sec_dev = sec // PER
-    code = (sec - sec_dev * PER) * BLOCK + first_v[...] + 1
-    slot = lax.broadcasted_iota(jnp.int32, (NSPACE, 16), 1)
-    dev = lax.broadcasted_iota(jnp.int32, (NSPACE, 16), 0)
-    match = (slot < count_v[...]) & (sec_dev == dev)
-    picked = jnp.sum(jnp.where(match, code, 0), axis=1, keepdims=True)
-    codes[...] = jnp.broadcast_to(picked, (NSPACE, BLOCK))[:, None, :]
+    slot = lax.broadcasted_iota(jnp.int32, (1, 16), 1)
+    listed = jnp.where(slot < count_v[...], first_v[...] + BLOCK * second_v[...] + 1, 0)
+    table[core, x, z] = jnp.zeros((1, BLOCK), jnp.int32)
+    table[core, x, z, :, 0:16] = listed
 
     for k in range(NB):
         j = k % GROUP - GROUP // 2
         row = weight[k:k + 1, :].astype(jnp.float32) * (2.0 ** (-j * j * DELTA * DELTA))
         wb[k] = jnp.broadcast_to(row, (16, CH)).astype(jnp.bfloat16)
 
-    pl.semaphore_wait(barrier, NSPACE - 1 + 2)
+    pl.semaphore_wait(barrier, 9)
 
     def ev(flow, i):
         da, db, (r0, n), sa, sb = EVENTS[i]
@@ -143,9 +142,15 @@
         src = feat.at[pl.ds(first_row, n // BLOCK)] if da == 0 and db == 0 else blocks
         return remote(src, blocks, gs.at[flow, i], gr.at[flow, i], to)
 
-    def code_copy(i):
-        to = lax.rem(me + i, NSPACE)
-        return remote(codes.at[to], codes_in.at[me], ks.at[i], kr.at[i], to)
+    def table_x(i):
+        mine = table.at[core, x, z]
+        return remote(mine, mine, ks.at[i], kr.at[i], xpeers[i])
+
+    def table_z(i):
+        mine = table.at[core, :, z]
+        return remote(mine, mine, ks.at[3 + i], kr.at[3 + i], zpeers[i])
+
+    table_core = remote(table.at[core], table.at[core], ks.at[6], kr.at[6], partner)
 
     def to_partner(c):
         blocks = g.at[pl.ds((c * NCORE + core) * PER, PER)]
@@ -168,11 +173,8 @@
     own_out = remote(feat, g.at[pl.ds(me * PER, PER)], ps.at[NX * NZ], pr.at[NX * NZ], partner)
     own_out.start()
 
-    @pl.loop(1, NSPACE)
-    def _(i):
-        code_copy(i).start()
-    own_code = pltpu.make_async_copy(codes.at[me], codes_in.at[me], ls.at[1])
-    own_code.start()
+    for i in range(3):
+        table_x(i).start()
 
     for a in range(3):
         for b in range(PER):
@@ -180,6 +182,11 @@
             posb[a, b] = jnp.broadcast_to(pos[a:a + 1, at], (BLOCK, BLOCK)).T
         at = pl.ds(pl.multiple_of(core * 512 + (chip // 4) * BLOCK, BLOCK), BLOCK)
         wt[a] = jnp.broadcast_to(wave[a:a + 1, at].astype(jnp.float32), (BLOCK, BLOCK)).T
+
+    for i in range(3):
+        table_x(i).wait_recv()
+    for i in range(3):
+        table_z(i).start()
 
     @pl.loop(0, NSPACE * PER // 8)
     def _(i):
@@ -216,7 +223,7 @@
             off = jnp.abs(there[a:a + 1, :] - posb[a, target])
             off = jnp.minimum(off, 8.0 - off)
             total = off * off if total is None else total + off * off
-        return jnp.sqrt(total) * SCALE
+        return jnp.sqrt(total) * (SCALE * 2.0 * DELTA)
 
     def half_pair(target, source, f32_rows):
         es = expansion(distance(target, source))
@@ -247,7 +254,7 @@
         s_acc[...] += jnp.dot(jnp.concatenate(blocks, 1), rows, preferred_element_type=jnp.float32)
 
     def slot_of(e):
-        value = code_s[e, 0, 0]
+        value = code_s[lax.rem(e, NCORE) * (NX * NZ) + e // NCORE, 0, 0]
         v = jnp.maximum(value - 1, 0)
         return value, v // BLOCK, lax.rem(v, BLOCK)
 
@@ -308,6 +315,9 @@
         both(c)
         add_factors(c)
 
+    for i in range(3):
+        table_z(i).wait_recv()
+    table_core.start()
     own.wait()
     own_out.wait_recv()
     add_factors(chip)
@@ -317,11 +327,11 @@
     start(14, 15)
     forward(near)
 
-    @pl.loop(1, NSPACE)
-    def _(i):
-        code_copy(i).wait_recv()
-    own_code.wait()
-    to_smem = pltpu.make_async_copy(codes_in, code_s, ls.at[2])
+    table_core.wait_recv()
+    rows = table[...].reshape(NSPACE, 1, BLOCK) - me * (PER * BLOCK)
+    hit = jnp.where((rows > 0) & (rows <= PER * BLOCK), rows, 0)
+    codes[...] = jnp.broadcast_to(jnp.sum(hit, axis=2, keepdims=True), (NSPACE, 1, BLOCK))
+    to_smem = pltpu.make_async_copy(codes, code_s, ls.at[2])
     to_smem.start()
     to_smem.wait()
     arrived(4, 7)
@@ -345,6 +355,7 @@
     forward(((2, 2),))
     pl.loop(0, 4)(knight_factors)
     early(chip_at(1, -1), chip_at(-1, 1))
+    early(chip_at(2, 0), chip_at(0, 2))
     both(chip_at(2, 2))
     add_factors(chip_at(2, 2))
 
@@ -352,27 +363,38 @@
     q = (2.0 * math.pi / 8.0) ** 2 * (n[0] * n[0] + n[1] * n[1] + n[2] * n[2])
     sm = smear[...]
     kern = (4.0 * math.pi / q) * jnp.exp(-0.5 * q * (sm * sm))
-    fg[core, 0, chip] = (s_acc[0:32, :] * kern).astype(jnp.bfloat16)
-    fg[core, 1, chip] = (s_acc[32:64, :] * kern).astype(jnp.bfloat16)
-
-    def f_copy(i):
-        own_f = fg.at[core, :, chip]
-        return remote(own_f, own_f, fs.at[i], fr.at[i], lax.rem(me + i, NSPACE))
-
-    @pl.loop(1, NSPACE)
-    def _(i):
-        f_copy(i).start()
-
-    @pl.loop(0, 8)
-    def _(i):
-        late, last = i // 4, i // 7
-        dx = 2 * (1 - late) + late * ((i - 4) + (i - 4) // 2 - last)
-        c = chip_at(dx, (1 - late) * i + late * (2 + last))
+    fg[core, 0, x, z] = (s_acc[0:32, :] * kern).astype(jnp.bfloat16)
+    fg[core, 1, x, z] = (s_acc[32:64, :] * kern).astype(jnp.bfloat16)
+
+    def f_x(i):
+        mine = fg.at[core, :, x, z]
+        return remote(mine, mine, fs.at[i], fr.at[i], xpeers[i])
+
+    def f_z(i):
+        mine = fg.at[core, :, :, z]
+        return remote(mine, mine, fs.at[3 + i], fr.at[3 + i], zpeers[i])
+
+    f_core = remote(fg.at[core], fg.at[core], fs.at[6], fr.at[6], partner)
+    for i in range(3):
+        f_x(i).start()
+
+    def late_step(i):
+        late, last = i // 3, i // 5
+        c = chip_at(2 * (1 - late) + late * (1 + 2 * (i - 3) - 2 * last), (1 - late) * (1 + i) + late * (2 + last))
         add_pairs([loaded_block(c * NCORE), loaded_block(c * NCORE + 1), own_slot(2 * i), own_slot(2 * i + 1)])
 
-    @pl.loop(1, NSPACE)
-    def _(i):
-        f_copy(i).wait_recv()
+    pl.loop(0, 2)(late_step)
+    for i in range(3):
+        f_x(i).wait_recv()
+    for i in range(3):
+        f_z(i).start()
+    pl.loop(2, 5)(late_step)
+    for i in range(3):
+        f_z(i).wait_recv()
+    f_core.start()
+    late_step(5)
+    add_pairs([own_slot(s) for s in range(12, 16)])
+    f_core.wait_recv()
 
     def message(b):
         at = pl.ds(b * BLOCK, BLOCK)
@@ -432,10 +454,11 @@
     for c in ups + downs + relays:
         c.wait_send()
 
-    @pl.loop(1, NSPACE)
-    def _(i):
-        code_copy(i).wait_send()
-        f_copy(i).wait_send()
+    for i in range(3):
+        for c in (table_x(i), table_z(i), f_x(i), f_z(i)):
+            c.wait_send()
+    table_core.wait_send()
+    f_core.wait_send()
 
     @pl.loop(1, NX * NZ)
     def _(i):
@@ -453,10 +476,10 @@
         out_specs=VM,
         scratch_shapes=[
             pltpu.VMEM((NSPACE * PER, BLOCK, CH), bf16),
-            pltpu.VMEM((NSPACE, 1, BLOCK), jnp.int32),
+            pltpu.VMEM((NCORE, NX, NZ, 1, BLOCK), jnp.int32),
             pltpu.VMEM((NSPACE, 1, BLOCK), jnp.int32),
             pltpu.SMEM((NSPACE, 1, BLOCK), jnp.int32),
-            pltpu.VMEM((NCORE, 2, NX * NZ, 32, CH), bf16),
+            pltpu.VMEM((NCORE, 2, NX, NZ, 32, CH), bf16),
             pltpu.VMEM((ROWS, 2 * KV), bf16),
             pltpu.VMEM((ROWS, CH), f32),
             pltpu.VMEM((3, PER, BLOCK, BLOCK), f32),
@@ -466,9 +489,9 @@
             pltpu.VMEM((64, CH), f32),
             pltpu.VMEM((NCHAN, PER, BLOCK, CH), bf16),
             dma((2, NEV)), dma((2, NEV)),
-            dma((NSPACE,)), dma((NSPACE,)),
+            dma((7,)), dma((7,)),
             dma((NX * NZ + 1,)), dma((NX * NZ + 1,)),
-            dma((NSPACE,)), dma((NSPACE,)),
+            dma((7,)), dma((7,)),
             dma((3 * PER,)), dma((3 * PER,)),
             dma((3,)),
         ],

time: 57.7 us -> 58.8 us (1.019)
  Pallas kernels: 55.4 us -> 56.4 us
    pallas_call x1, Pallas kernels: 55.4 us -> 56.4 us  [body(): pl.pallas_call(kernel, out_shape=jax.ShapeDtypeStruct((ROWS, CH), bf16),...]
where the time goes in v4:
time: 58.8 us; the launch traced here: 58.7 us
  Pallas kernels  56.4 us (96%)
  local copies, waits for them, and re-layouts  1.57 us (3%)
  between operations  0.66 us (1%)
    pallas_call x1, Pallas kernels, body(): pl.pallas_call(kernel, out_shape=jax.ShapeDtypeStruct((ROWS, CH), bf16),...  56.4 us
    unnamed x1, local copies, waits for them, and re-layouts  1.57 us

profile of v4, /device:TPU:0, one launch (start us, length us, event | category | flops | bytes accessed | tf_op | source)
XLA Modules:
  0.0 58.7 jit_solution(12687534129001995889)
XLA Ops:
  0.7 56.4 %layer.1 = bf16[512,128]{1,0:T(8,128)(2,1)} custom-call(bf16[4,128,128]{2,1,0:T(8,128)(2,1)} %bitcast.6, s32[16]{0:T(128)} %first.1, s32[16]{0:T(128)} %second.1, s32[1]{0:T(128)} %copy.11.count, s32[1,16]{1,0:T(1,128)} %bitcast.7, s32[1,16]{1,0:T(1,128)} %bitcast.8, s32[1,1]{1,0:T(1,128)} %bitcast.5.count_v, f32[3,16384]{1,0:T(4,128)} %pos.1, ...), custom_call_target="tpu_custom_call" | custom-call | tf_op jit(solution)/shard_map/layer/pallas_call | solution.py:472
  57.1 1.6 %copy.12 = bf16[512,128]{1,0:T(8,128)(2,1)} copy(bf16[512,128]{1,0:T(8,128)(2,1)} %layer.1) | data formatting | bytes 262144

commit v5 on v4

--- a/solution.py
+++ b/solution.py
@@ -84,15 +84,15 @@
         mid = jnp.exp2(a * (centre * shrink - dk))
         up, down = jnp.exp2(a), jnp.exp2(centre - d2)
         out[c] = mid
-        e = mid
-        for j in range(1, GROUP - half):
-            e = e * up
-            out[c + j] = e
-        e = mid
-        for j in range(1, half + 1):
-            e = e * down
-            out[c - j] = e
-    return [e.astype(jnp.bfloat16) for e in out]
+        for sign, ratio, length in ((1, up, GROUP - half - 1), (-1, down, half)):
+            e = mid
+            for j in range(1, length + 1):
+                if j == 3:
+                    e, ratio = out[c + 2 * sign], ratio.astype(jnp.bfloat16)
+                e = e * ratio
+                out[c + sign * j] = e.astype(jnp.bfloat16)
+        out[c] = mid.astype(jnp.bfloat16)
+    return out
 
 
 def kernel(feat, first, second, count, first_v, second_v, count_v, pos, wave, weight, smear, mix, out,
@@ -169,12 +169,11 @@
     def chip_at(dx, dz):
         return lax.rem(x + dx + NX, NX) * NZ + lax.rem(z + dz + NZ, NZ)
 
+    for i in range(3):
+        table_x(i).start()
     start(0, 1, 2, 3)
     own_out = remote(feat, g.at[pl.ds(me * PER, PER)], ps.at[NX * NZ], pr.at[NX * NZ], partner)
     own_out.start()
-
-    for i in range(3):
-        table_x(i).start()
 
     for a in range(3):
         for b in range(PER):
@@ -182,11 +181,6 @@
             posb[a, b] = jnp.broadcast_to(pos[a:a + 1, at], (BLOCK, BLOCK)).T
         at = pl.ds(pl.multiple_of(core * 512 + (chip // 4) * BLOCK, BLOCK), BLOCK)
         wt[a] = jnp.broadcast_to(wave[a:a + 1, at].astype(jnp.float32), (BLOCK, BLOCK)).T
-
-    for i in range(3):
-        table_x(i).wait_recv()
-    for i in range(3):
-        table_z(i).start()
 
     @pl.loop(0, NSPACE * PER // 8)
     def _(i):
@@ -265,11 +259,10 @@
     def chosen_block(e):
         value, target, source = slot_of(e)
         local = jnp.where(value > 0, source - e * PER, -1)
-        f = None
+        f = jnp.zeros((BLOCK, CH), jnp.bfloat16)
         for b in range(PER):
-            block = jnp.where(local == b, g[e * PER + b].astype(jnp.float32), 0.0)
-            f = block if f is None else f + block
-        return target, source, f
+            f = jnp.where(local == b, g[e * PER + b], f)
+        return target, source, f.astype(jnp.float32)
 
     def loaded_block(e):
         value, target, source = slot_of(e)
@@ -316,8 +309,9 @@
         add_factors(c)
 
     for i in range(3):
-        table_z(i).wait_recv()
-    table_core.start()
+        table_x(i).wait_recv()
+    for i in range(3):
+        table_z(i).start()
     own.wait()
     own_out.wait_recv()
     add_factors(chip)
@@ -327,6 +321,17 @@
     start(14, 15)
     forward(near)
 
+    arrived(4, 7)
+    start(10, 11, 12, 13)
+    pl.loop(0, 4)(near_factors)
+    for i in range(3):
+        table_z(i).wait_recv()
+    table_core.start()
+    arrived(5, 6, 8, 9)
+    start(16, 17, 18, 19)
+    forward(diag)
+    arrived(14, 15)
+    forward(far)
     table_core.wait_recv()
     rows = table[...].reshape(NSPACE, 1, BLOCK) - me * (PER * BLOCK)
     hit = jnp.where((rows > 0) & (rows <= PER * BLOCK), rows, 0)
@@ -334,14 +339,6 @@
     to_smem = pltpu.make_async_copy(codes, code_s, ls.at[2])
     to_smem.start()
     to_smem.wait()
-    arrived(4, 7)
-    start(10, 11, 12, 13)
-    pl.loop(0, 4)(near_factors)
-    arrived(5, 6, 8, 9)
-    start(16, 17, 18, 19)
-    forward(diag)
-    arrived(14, 15)
-    forward(far)
     early(chip, chip_at(1, 0))
     arrived(10, 13)
     start(20, 21)

time: 58.8 us -> 55.9 us (0.951)
  Pallas kernels: 56.4 us -> 53.6 us
    pallas_call x1, Pallas kernels: 56.4 us -> 53.6 us  [body(): pl.pallas_call(kernel, out_shape=jax.ShapeDtypeStruct((ROWS, CH), bf16),...]
where the time goes in v5:
time: 55.9 us; the launch traced here: 55.8 us
  Pallas kernels  53.6 us (96%)
  local copies, waits for them, and re-layouts  1.57 us (3%)
  between operations  0.66 us (1%)
    pallas_call x1, Pallas kernels, body(): pl.pallas_call(kernel, out_shape=jax.ShapeDtypeStruct((ROWS, CH), bf16),...  53.6 us
    unnamed x1, local copies, waits for them, and re-layouts  1.57 us

profile of v5, /device:TPU:0, one launch (start us, length us, event | category | flops | bytes accessed | tf_op | source)
XLA Modules:
  0.0 55.8 jit_solution(11442756998392679005)
XLA Ops:
  0.7 53.6 %layer.1 = bf16[512,128]{1,0:T(8,128)(2,1)} custom-call(bf16[4,128,128]{2,1,0:T(8,128)(2,1)} %bitcast.6, s32[16]{0:T(128)} %first.1, s32[16]{0:T(128)} %second.1, s32[1]{0:T(128)} %copy.11.count, s32[1,16]{1,0:T(1,128)} %bitcast.7, s32[1,16]{1,0:T(1,128)} %bitcast.8, s32[1,1]{1,0:T(1,128)} %bitcast.5.count_v, f32[3,16384]{1,0:T(4,128)} %pos.1, ...), custom_call_target="tpu_custom_call" | custom-call | tf_op jit(solution)/shard_map/layer/pallas_call | solution.py:469
  54.2 1.6 %copy.12 = bf16[512,128]{1,0:T(8,128)(2,1)} copy(bf16[512,128]{1,0:T(8,128)(2,1)} %layer.1) | data formatting | bytes 262144

commit v6 on v5

--- a/solution.py
+++ b/solution.py
@@ -124,11 +124,6 @@
     table[core, x, z] = jnp.zeros((1, BLOCK), jnp.int32)
     table[core, x, z, :, 0:16] = listed
 
-    for k in range(NB):
-        j = k % GROUP - GROUP // 2
-        row = weight[k:k + 1, :].astype(jnp.float32) * (2.0 ** (-j * j * DELTA * DELTA))
-        wb[k] = jnp.broadcast_to(row, (16, CH)).astype(jnp.bfloat16)
-
     pl.semaphore_wait(barrier, 9)
 
     def ev(flow, i):
@@ -174,6 +169,11 @@
     start(0, 1, 2, 3)
     own_out = remote(feat, g.at[pl.ds(me * PER, PER)], ps.at[NX * NZ], pr.at[NX * NZ], partner)
     own_out.start()
+
+    for k in range(NB):
+        j = k % GROUP - GROUP // 2
+        row = weight[k:k + 1, :].astype(jnp.float32) * (2.0 ** (-j * j * DELTA * DELTA))
+        wb[k] = jnp.broadcast_to(row, (16, CH)).astype(jnp.bfloat16)
 
     for a in range(3):
         for b in range(PER):

time: 55.9 us -> 55.9 us (level)
  no operation moved by 1% of the time
where the time goes in v6:
time: 55.9 us; the launch traced here: 55.8 us
  Pallas kernels  53.6 us (96%)
  local copies, waits for them, and re-layouts  1.57 us (3%)
  between operations  0.66 us (1%)
    pallas_call x1, Pallas kernels, body(): pl.pallas_call(kernel, out_shape=jax.ShapeDtypeStruct((ROWS, CH), bf16),...  53.6 us
    unnamed x1, local copies, waits for them, and re-layouts  1.57 us

profile of v6, /device:TPU:0, one launch (start us, length us, event | category | flops | bytes accessed | tf_op | source)
XLA Modules:
  0.0 55.8 jit_solution(7643004173563416854)
XLA Ops:
  0.7 53.6 %layer.1 = bf16[512,128]{1,0:T(8,128)(2,1)} custom-call(bf16[4,128,128]{2,1,0:T(8,128)(2,1)} %bitcast.6, s32[16]{0:T(128)} %first.1, s32[16]{0:T(128)} %second.1, s32[1]{0:T(128)} %copy.11.count, s32[1,16]{1,0:T(1,128)} %bitcast.7, s32[1,16]{1,0:T(1,128)} %bitcast.8, s32[1,1]{1,0:T(1,128)} %bitcast.5.count_v, f32[3,16384]{1,0:T(4,128)} %pos.1, ...), custom_call_target="tpu_custom_call" | custom-call | tf_op jit(solution)/shard_map/layer/pallas_call | solution.py:469
  54.2 1.6 %copy.12 = bf16[512,128]{1,0:T(8,128)(2,1)} copy(bf16[512,128]{1,0:T(8,128)(2,1)} %layer.1) | data formatting | bytes 262144

commit v7 on v5

--- a/solution.py
+++ b/solution.py
@@ -87,8 +87,8 @@
         for sign, ratio, length in ((1, up, GROUP - half - 1), (-1, down, half)):
             e = mid
             for j in range(1, length + 1):
-                if j == 3:
-                    e, ratio = out[c + 2 * sign], ratio.astype(jnp.bfloat16)
+                if j == 2:
+                    e, ratio = out[c + sign], ratio.astype(jnp.bfloat16)
                 e = e * ratio
                 out[c + sign * j] = e.astype(jnp.bfloat16)
         out[c] = mid.astype(jnp.bfloat16)

time: 55.9 us -> 55.4 us (level)
  Pallas kernels: 53.6 us -> 53 us
    pallas_call x1, Pallas kernels: 53.6 us -> 53 us  [body(): pl.pallas_call(kernel, out_shape=jax.ShapeDtypeStruct((ROWS, CH), bf16),...]
where the time goes in v7:
time: 55.4 us; the launch traced here: 55.2 us
  Pallas kernels  53 us (96%)
  local copies, waits for them, and re-layouts  1.57 us (3%)
  between operations  0.66 us (1%)
    pallas_call x1, Pallas kernels, body(): pl.pallas_call(kernel, out_shape=jax.ShapeDtypeStruct((ROWS, CH), bf16),...  53 us
    unnamed x1, local copies, waits for them, and re-layouts  1.57 us

profile of v7, /device:TPU:0, one launch (start us, length us, event | category | flops | bytes accessed | tf_op | source)
XLA Modules:
  0.0 55.2 jit_solution(11428446435085713593)
XLA Ops:
  0.7 53.0 %layer.1 = bf16[512,128]{1,0:T(8,128)(2,1)} custom-call(bf16[4,128,128]{2,1,0:T(8,128)(2,1)} %bitcast.6, s32[16]{0:T(128)} %first.1, s32[16]{0:T(128)} %second.1, s32[1]{0:T(128)} %copy.11.count, s32[1,16]{1,0:T(1,128)} %bitcast.7, s32[1,16]{1,0:T(1,128)} %bitcast.8, s32[1,1]{1,0:T(1,128)} %bitcast.5.count_v, f32[3,16384]{1,0:T(4,128)} %pos.1, ...), custom_call_target="tpu_custom_call" | custom-call | tf_op jit(solution)/shard_map/layer/pallas_call | solution.py:469
  53.6 1.6 %copy.12 = bf16[512,128]{1,0:T(8,128)(2,1)} copy(bf16[512,128]{1,0:T(8,128)(2,1)} %layer.1) | data formatting | bytes 262144
